TPU v7x, 256 devices: a whole 4x4x8 slice. The times are simulated.
256 devices in a mesh: col: 32 (over z, y), row: 8 (over x, core).
Axes of the slice: x: 4, y: 4, z: 8, core: 2. Of those that a mesh axis runs over, the one named last changes fastest.
Arguments:
- panel: float32 [2, 12288, 6144], P(None, 'row', 'col'), may hold values from -0.078125 to 0.078125
- prior: float32 [6144, 64], P('col'), may hold values from -6 to 6
- right_side: float32 [2, 12288, 64], P(None, 'row'), may hold values from -6 to 6
- coupling: float32 [12288, 12288], P('row', 'col'), may hold values from -0.0546875 to 0.0546875
- inverses: float32 [2, 12288, 12288], P(None, 'row', 'col'), as said below
Outputs:
- solved: float32 [2, 12288, 64], P(None, 'row')
Inputs may be any that keep to these rules, and one draw needn't show every extreme that they name: `inverses`: each of the two blocks is zero above its diagonal, and its diagonal lies between 0.5 and 2.
All inputs are finite; a program needn't handle non-finite values.
Results may differ from a plain program's by a relative error of at most 0.00011.
Values sent between devices are 32-bit elements; how exact they have to be, the bound alone decides.
No kernel may reach another device: no remote copies, remote signals or barrier semaphores. Data moves between devices by JAX's collectives and lax.ppermute only.
A program may use at most 64 MiB of HBM per device.

v0:
```python
import jax
import jax.numpy as jnp
from jax import lax
from jax.sharding import PartitionSpec as P


def split_up(array, dim, peers):
    before, after = (array.shape[:dim], array.shape[dim + 1 :])
    return jnp.moveaxis(array.reshape(*before, peers, -1, *after), dim, 0)


def sum_at_owner(array, axis, dim):
    parts = split_up(array, dim, lax.axis_size(axis))
    arrived = lax.all_to_all(parts, axis, split_axis=0, concat_axis=0, tiled=True)
    return arrived.sum(axis=0)


def filled_up(lines, peers):
    spare = -lines.shape[0] % peers
    if not spare:
        return lines
    return jnp.concatenate([lines, jnp.zeros((spare, *lines.shape[1:]), lines.dtype)])


def joined_along(parts, dim):
    dims = list(parts.shape[1:])
    dims[dim] *= parts.shape[0]
    return jnp.moveaxis(parts, 0, dim).reshape(dims)


def sent_to_all(array, axis):
    copies = jnp.broadcast_to(array, (lax.axis_size(axis), *array.shape))
    return lax.all_to_all(copies, axis, split_axis=0, concat_axis=0, tiled=True)


def gathered_copies(array, axis, dim):
    return joined_along(sent_to_all(array, axis), dim)


def nested_sum(array, axes):
    lines = array.reshape(-1, array.shape[-1])
    own = sum_at_owner(filled_up(lines, lax.axis_size(axes)), axes, 0)
    whole = gathered_copies(own, axes, 0)
    return whole[: len(lines)].reshape(array.shape)


def from_root(array, axis, root):
    return lax.dynamic_index_in_dim(lax.all_gather(array, axis), root, 0, keepdims=False)


def settle(partial_value, base, width):
    tile_rows = partial_value.shape[0]
    tile = base - nested_sum(partial_value, "col")
    offset = lax.axis_index("col") * width
    local = lax.dynamic_slice_in_dim(tile, offset % tile_rows, width, 0)
    segment = from_root(local, "row", offset // tile_rows)
    return (tile, segment)


def shards(panel, prior, right_side, coupling, inverses):
    highest = lax.Precision.HIGHEST
    width = inverses.shape[2]
    carried = jnp.einsum("bik,kr->bir", panel, prior, precision=highest)
    zeros = jnp.zeros_like(right_side[0])
    first_tile, first_segment = settle(carried[0], right_side[0], width)
    leading_part = jnp.dot(inverses[0], first_segment, precision=highest)
    leading, leading_segment = settle(-leading_part, zeros, width)
    second_part = carried[1] + jnp.dot(coupling, leading_segment, precision=highest)
    second_tile, second_segment = settle(second_part, right_side[1], width)
    trailing_part = jnp.dot(inverses[1], second_segment, precision=highest)
    trailing = nested_sum(trailing_part, "col")
    return jnp.stack([leading, trailing])


def solution(mesh):
    in_specs = (
        P(None, "row", "col"),
        P("col", None),
        P(None, "row", None),
        P("row", "col"),
        P(None, "row", "col"),
    )
    out_specs = P(None, "row", None)
    return jax.shard_map(shards, mesh=mesh, in_specs=in_specs, out_specs=out_specs, check_vma=False)
```

profile of v0, /device:TPU:8, one launch (start us, length us, event | category | flops | bytes accessed | tf_op | source)
XLA Modules:
  0.0 268.4 jit_solution(6501843347263199051)
XLA Ops:
  0.0 1.7 copy-done
  1.7 2.5 fusion.22
  5.9 25.5 %all_to_all.40 = f32[32,1,3072]{2,1,0:T(1,128)S(1)} all-to-all(f32[32,1,3072]{2,1,0:T(1,128)S(1)} %reshape.39), channel_id=1, replica_groups=mesh['col'=32,'row'=8] {'col'}, dimensions={0} | all-to-all | bytes 786432 | tf_op jit(solution)/shard_map/all_to_all | solution.py:14
  32.0 1.5 reduce
  33.9 1.2 reshape.41
  35.1 5.6 %all-to-all-start.1 = ((f32[32,1,3072]{2,1,0:T(1,128)}), f32[32,1,3072]{2,1,0:T(1,128)S(1)}, u32[]{:S(2)}, u32[]{:S(2)}) async-start(f32[32,1,3072]{2,1,0:T(1,128)} %reshape.41), calls=%async_computation.1 | async-start | bytes 786432 | tf_op jit(solution)/shard_map/all_to_all | solution.py:33
  40.7 1.9 slice_bitcast_fusion.1
  42.6 11.3 %all-to-all-done.1 = f32[32,1,3072]{2,1,0:T(1,128)S(1)} async-done(((f32[32,1,3072]{2,1,0:T(1,128)}), f32[32,1,3072]{2,1,0:T(1,128)S(1)}, u32[]{:S(2)}, u32[]{:S(2)}) %all-to-all-start.1) | async-done | bytes 393248 | tf_op jit(solution)/shard_map/all_to_all | solution.py:33
  53.9 1.5 reduce.1
  55.5 1.1 reshape.42
  56.6 0.9 constant_dynamic-slice_fusion.5
  57.8 13.8 %all-gather = f32[3072,64]{0,1:T(8,128)S(1)} all-gather(f32[384,64]{0,1:T(8,128)S(1)} %dynamic-slice_subtract_fusion.1), channel_id=2, replica_groups=mesh['col'=32,'row'=8] {'row'}, dimensions={0}, use_global_device_ids=true | all-gather | bytes 884736 | tf_op jit(solution)/shard_map/all_gather | solution.py:48
  71.7 4.1 %fusion.9 = f32[1536,64]{0,1:T(8,128)S(1)} fusion(f32[2,1536,384]{2,1,0:T(8,128)} %param.9, f32[1,384,64]{1,0,2:T(1,128)S(1)} %constant_dynamic-slice_fusion.4), kind=kOutput, calls=%fused_computation.7 | convolution fusion | flops 453083136 | bytes 2850816 | tf_op jit(solution)/shard_map/dot_general | solution.py:66
  76.6 19.9 %all_to_all.41 = f32[32,1,3072]{2,1,0:T(1,128)S(1)} all-to-all(f32[32,1,3072]{2,1,0:T(1,128)S(1)} %reshape.43), channel_id=1, replica_groups=mesh['col'=32,'row'=8] {'col'}, dimensions={0} | all-to-all | bytes 786432 | tf_op jit(solution)/shard_map/all_to_all | solution.py:14
  96.5 1.5 reduce.2
  98.9 18.7 %all_to_all.42 = f32[32,1,3072]{2,1,0:T(1,128)S(1)} all-to-all(f32[32,1,3072]{2,1,0:T(1,128)S(1)} %reshape.45), channel_id=1, replica_groups=mesh['col'=32,'row'=8] {'col'}, dimensions={0} | all-to-all | bytes 786432 | tf_op jit(solution)/shard_map/all_to_all | solution.py:33
  117.6 1.5 reduce.3
  119.1 1.1 reshape.46
  120.2 1.2 broadcast_subtract_fusion
  121.5 13.5 %all-gather.1 = f32[3072,64]{0,1:T(8,128)S(1)} all-gather(f32[384,64]{0,1:T(8,128)S(1)} %copy.27), channel_id=3, replica_groups=mesh['col'=32,'row'=8] {'row'}, dimensions={0}, use_global_device_ids=true | all-gather | bytes 884736 | tf_op jit(solution)/shard_map/all_gather | solution.py:48
  135.3 4.1 %fusion.15 = f32[1536,64]{0,1:T(8,128)S(1)} fusion(f32[1536,384]{1,0:T(8,128)} %param.8, f32[2,1536,64]{1,2,0:T(8,128)S(1)} %copy-done.2, f32[1,384,64]{1,0,2:T(1,128)S(1)} %constant_dynamic-slice_fusion.2), kind=kOutput, calls=%fused_computation.10 | convolution fusion | flops 453083136 | bytes 3244032 | tf_op jit(solution)/shard_map/dot_general | solution.py:68
  139.4 1.2 copy.20
  140.6 1.6 reshape.47
  142.2 20.0 %all_to_all.43 = f32[32,1,3072]{2,1,0:T(1,128)} all-to-all(f32[32,1,3072]{2,1,0:T(1,128)S(1)} %reshape.47), channel_id=1, replica_groups=mesh['col'=32,'row'=8] {'col'}, dimensions={0} | all-to-all | bytes 786432 | tf_op jit(solution)/shard_map/all_to_all | solution.py:14
  162.2 2.5 reduce.4
  164.7 1.1 reshape.48
  165.8 1.2 reduce_sum.38
  168.0 1.6 reshape.49
  169.6 18.8 %all_to_all.44 = f32[32,1,3072]{2,1,0:T(1,128)} all-to-all(f32[32,1,3072]{2,1,0:T(1,128)S(1)} %reshape.49), channel_id=1, replica_groups=mesh['col'=32,'row'=8] {'col'}, dimensions={0} | all-to-all | bytes 786432 | tf_op jit(solution)/shard_map/all_to_all | solution.py:33
  188.4 2.5 reduce.5
  190.9 1.1 reshape.50
  193.1 1.0 dynamic-slice_subtract_fusion
  194.1 13.6 %all-gather.2 = f32[3072,64]{0,1:T(8,128)S(1)} all-gather(f32[384,64]{0,1:T(8,128)S(1)} %dynamic-slice_subtract_fusion), channel_id=4, replica_groups=mesh['col'=32,'row'=8] {'row'}, dimensions={0}, use_global_device_ids=true | all-gather | bytes 884736 | tf_op jit(solution)/shard_map/all_gather | solution.py:48
  207.9 4.1 %fusion.12 = f32[1536,64]{0,1:T(8,128)S(1)} fusion(f32[2,1536,384]{2,1,0:T(8,128)} %param.9, f32[1,384,64]{1,0,2:T(1,128)S(1)} %constant_dynamic-slice_fusion), kind=kOutput, calls=%fused_computation.8 | convolution fusion | flops 452984832 | bytes 2850816 | tf_op jit(solution)/shard_map/dot_general | solution.py:70
  212.0 1.2 copy.22
  213.2 1.6 reshape.51
  214.8 20.0 %all_to_all.45 = f32[32,1,3072]{2,1,0:T(1,128)} all-to-all(f32[32,1,3072]{2,1,0:T(1,128)S(1)} %reshape.51), channel_id=1, replica_groups=mesh['col'=32,'row'=8] {'col'}, dimensions={0} | all-to-all | bytes 786432 | tf_op jit(solution)/shard_map/all_to_all | solution.py:14
  234.8 2.5 reduce.6
  237.4 1.1 reshape.52
  238.4 1.2 reduce_sum.39
  240.6 2.4 reshape.53
  243.0 5.6 %all-to-all-start.7 = ((f32[32,1,3072]{2,1,0:T(1,128)}), f32[32,1,3072]{2,1,0:T(1,128)S(1)}, u32[]{:S(2)}, u32[]{:S(2)}) async-start(f32[32,1,3072]{2,1,0:T(1,128)} %reshape.53), calls=%async_computation.7 | async-start | bytes 786432 | tf_op jit(solution)/shard_map/all_to_all | solution.py:33
  248.5 1.0 copy.18
  249.5 12.3 %all-to-all-done.7 = f32[32,1,3072]{2,1,0:T(1,128)S(1)} async-done(((f32[32,1,3072]{2,1,0:T(1,128)}), f32[32,1,3072]{2,1,0:T(1,128)S(1)}, u32[]{:S(2)}, u32[]{:S(2)}) %all-to-all-start.7) | async-done | bytes 393248 | tf_op jit(solution)/shard_map/all_to_all | solution.py:33
  261.8 2.4 reduce.7
  264.2 1.2 reshape.54
  265.4 1.0 copy.23
  266.4 1.9 pad_maximum_fusion
  (34 shorter events, 8.0 us)
Async XLA Ops:
  0.0 1.7 copy-start
  4.2 0.9 copy-start.1
  35.1 18.9 %all-to-all-start.1 = ((f32[32,1,3072]{2,1,0:T(1,128)}), f32[32,1,3072]{2,1,0:T(1,128)S(1)}, u32[]{:S(2)}, u32[]{:S(2)}) async-start(f32[32,1,3072]{2,1,0:T(1,128)} %reshape.41), calls=%async_computation.1 | async-start | bytes 786432 | tf_op jit(solution)/shard_map/all_to_all | solution.py:33
  121.5 13.8 %copy-start.2 = (f32[2,1536,64]{1,2,0:T(8,128)S(1)}, f32[2,1536,64]{1,2,0:T(8,128)}, u32[]{:S(2)}) copy-start(f32[2,1536,64]{1,2,0:T(8,128)} %copy-done.1) | copy-start | bytes 2359300
  243.0 18.9 %all-to-all-start.7 = ((f32[32,1,3072]{2,1,0:T(1,128)}), f32[32,1,3072]{2,1,0:T(1,128)S(1)}, u32[]{:S(2)}, u32[]{:S(2)}) async-start(f32[32,1,3072]{2,1,0:T(1,128)} %reshape.53), calls=%async_computation.7 | async-start | bytes 786432 | tf_op jit(solution)/shard_map/all_to_all | solution.py:33
  264.2 2.3 copy-start.3
where the time goes:
time: 271 us; the launch traced here: 268 us
  blocking collectives  164 us (61%)
  local copies, waits for them, and re-layouts  31.8 us (12%)
  waiting for transfers between devices  23.6 us (9%)
  other arithmetic  22.9 us (8%)
  matrix products  14.8 us (5%)
  starting transfers between devices  11.1 us (4%)
    all_to_all x4, blocking collectives, sum_at_owner(): lax.all_to_all(parts, axis, split_axis=0, concat_axis=0, tiled=True)  85.4 us
    all_gather x3, blocking collectives, from_root(): lax.all_gather(array, axis)  40.9 us
    all_to_all x2, blocking collectives, sent_to_all(): return lax.all_to_all(copies, axis, split_axis=0, concat_axis=0, tiled=True)  37.4 us
    all_to_all x2, waiting for transfers between devices, sent_to_all(): return lax.all_to_all(copies, axis, split_axis=0, concat_axis=0, tiled=True)  23.6 us
    unnamed x30, local copies, waits for them, and re-layouts  20.3 us
    all_to_all x2, starting transfers between devices, sent_to_all(): return lax.all_to_all(copies, axis, split_axis=0, concat_axis=0, tiled=True)  11.1 us
    all_to_all x4, other arithmetic, sum_at_owner(): lax.all_to_all(parts, axis, split_axis=0, concat_axis=0, tiled=True)  8.18 us
    all_to_all x4, other arithmetic, sent_to_all(): return lax.all_to_all(copies, axis, split_axis=0, concat_axis=0, tiled=True)  7.99 us
  transfers between devices with their start and end apart: 2, of which 2 were waited for; matrix products, arithmetic and copies ran while one was open for 1% of the time, Pallas kernels for 0%

commit v1 on v0

v1 whole, which is shorter than its diff:
```python
import jax
import jax.numpy as jnp
from jax import lax
from jax.experimental import pallas as pl
from jax.experimental.pallas import tpu as pltpu
from jax.sharding import Mesh, PartitionSpec as P

ROW = ("x", "c")
COL = ("z", "y")
ALL = ("z", "y", "x", "c")
SLOT = (24, 128)
VMEM = pl.BlockSpec(memory_space=pltpu.VMEM)
HBM = pl.BlockSpec(memory_space=pltpu.HBM)


def grant(mib):
    return pltpu.CompilerParams(vmem_limit_bytes=mib << 20)


def halves(value):
    high = value.astype(jnp.bfloat16)
    low = (value - high.astype(jnp.float32)).astype(jnp.bfloat16)
    return high, low


def product(left, right, contract):
    left_high, left_low = halves(left)
    right_high, right_low = halves(right)
    dims = (((1,), (contract,)), ((), ()))
    both = lax.dot_general(
        jnp.concatenate([left_high, left_low], 0), right_high, dims, preferred_element_type=jnp.float32
    )
    rest = lax.dot_general(left_high, right_low, dims, preferred_element_type=jnp.float32)
    return both[:64] + (both[64:] + rest)


def put_slots(out_ref, value, start, add_ref=None):
    for at in range(value.shape[1] // 128):
        tile = start // 128 + at
        y, t = tile // 3, tile % 3
        for z in range(8):
            part = value[8 * z : 8 * z + 8, 128 * at : 128 * at + 128]
            if add_ref is not None:
                part = part + add_ref[4 * z + y, 8 * t : 8 * t + 8, :]
            out_ref[4 * z + y, 8 * t : 8 * t + 8, :] = part


def chunks(source, buffer, sems):
    copies = [pltpu.make_async_copy(source(g), buffer.at[g], sems.at[g]) for g in range(3)]
    for copy in copies:
        copy.start()
    for g in range(3):
        copies[g].wait()
        yield g


def carry_kernel(b, prior_ref, panel_ref, out_ref, buffer, sems):
    for g in chunks(lambda g: panel_ref.at[b, :, pl.ds(512 * g, 512)], buffer, sems):
        put_slots(out_ref, product(prior_ref[...], buffer[g], 0), 512 * g)


def carried(prior_t, panel_t, b):
    return pl.pallas_call(
        lambda *refs: carry_kernel(b, *refs),
        out_shape=jax.ShapeDtypeStruct((32, *SLOT), jnp.float32),
        in_specs=[VMEM, HBM],
        out_specs=VMEM,
        scratch_shapes=[pltpu.VMEM((3, 192, 512), jnp.float32), pltpu.SemaphoreType.DMA((3,))],
        compiler_params=grant(62),
        name=f"carry{b}",
    )(prior_t, panel_t)


def joined(gathered_ref):
    return jnp.concatenate(
        [jnp.concatenate([gathered_ref[e, 8 * t : 8 * t + 8, :] for t in range(3)], 1) for e in range(8)], 0
    )


def factor_kernel(b, gathered_ref, matrix_ref, *refs):
    *add, out_ref, buffer, sems = refs
    for g in chunks(lambda g: matrix_ref.at[b, pl.ds(512 * g, 512), :], buffer, sems):
        put_slots(out_ref, product(joined(gathered_ref), buffer[g], 1), 512 * g, *add)


def factor(gathered, matrix, b, *add):
    return pl.pallas_call(
        lambda *refs: factor_kernel(b, *refs),
        out_shape=jax.ShapeDtypeStruct((32, *SLOT), jnp.float32),
        in_specs=[VMEM, HBM] + [VMEM] * len(add),
        out_specs=VMEM,
        scratch_shapes=[pltpu.VMEM((3, 512, 384), jnp.float32), pltpu.SemaphoreType.DMA((3,))],
        compiler_params=grant(62),
        name="factor",
    )(gathered, matrix, *add)


def total_kernel(copies, parts_ref, *refs):
    out_ref = refs[-1]
    for t in range(3):
        rows = slice(8 * t, 8 * t + 8)
        sums = [parts_ref[k, rows, :] for k in range(4)]
        for s in range(4, 32):
            sums[s % 4] = sums[s % 4] + parts_ref[s, rows, :]
        value = (sums[0] + sums[1]) + (sums[2] + sums[3])
        if len(refs) > 1:
            value = refs[0][rows, :] - value
        for k in range(copies):
            out_ref[k, rows, :] = value


def total(parts, copies, base=None):
    args = [parts] if base is None else [parts, base]
    return pl.pallas_call(
        lambda *refs: total_kernel(copies, *refs),
        out_shape=jax.ShapeDtypeStruct((copies, *SLOT), jnp.float32),
        in_specs=[VMEM] * len(args),
        out_specs=VMEM,
        compiler_params=grant(4),
        name="total",
    )(*args)


def finish_kernel(leading_ref, trailing_ref, out_ref):
    for b, ref in enumerate((leading_ref, trailing_ref)):
        for z in range(8):
            for y in range(4):
                for t in range(3):
                    out_ref[b, 8 * z : 8 * z + 8, 384 * y + 128 * t : 384 * y + 128 * t + 128] = ref[
                        4 * z + y, 8 * t : 8 * t + 8, :
                    ]


def finish(leading, trailing):
    return pl.pallas_call(
        finish_kernel,
        out_shape=jax.ShapeDtypeStruct((2, 64, 1536), jnp.float32),
        in_specs=[VMEM] * 2,
        out_specs=VMEM,
        compiler_params=grant(8),
        name="finish",
    )(leading, trailing)


def exchanged(parts, axes):
    return lax.all_to_all(parts, axes, split_axis=0, concat_axis=0, tiled=True)


def device(z, y, row):
    return (z * 4 + y) * 8 + row


TURN = [(device(z, y, row), device(row, y, z)) for z in range(8) for y in range(4) for row in range(8)]


def spread(piece):
    turned = lax.ppermute(piece, ALL, TURN)
    return exchanged(jnp.broadcast_to(turned, (8, *SLOT)), ROW)


def shards(panel, prior, right_side, coupling, inverses):
    panel_t = panel.transpose(0, 2, 1)
    prior_t = prior.T
    right_t = right_side.transpose(0, 2, 1)
    z, y = lax.axis_index("z"), lax.axis_index("y")
    own = lax.dynamic_slice(right_t, (0, 8 * z, 384 * y), (2, 8, 384))
    own = own.reshape(2, 8, 3, 128).transpose(0, 2, 1, 3).reshape(2, *SLOT)

    first = total(exchanged(carried(prior_t, panel_t, 0), COL), 1, own[0])
    later = carried(prior_t, panel_t, 1)
    leading_parts = factor(spread(first), inverses, 0)
    leading = total(exchanged(leading_parts, COL), 1)
    second_parts = factor(spread(leading), coupling[None], 0, later)
    second = total(exchanged(second_parts, COL), 1, own[1])
    leading_all = exchanged(jnp.broadcast_to(leading, (32, *SLOT)), COL)
    trailing_parts = factor(spread(second), inverses, 1)
    trailing = total(exchanged(trailing_parts, COL), 32)
    trailing_all = exchanged(trailing, COL)
    return finish(leading_all, trailing_all).transpose(0, 2, 1)


def solution(mesh):
    fine = Mesh(mesh.devices.reshape(8, 4, 4, 2), ALL)
    in_specs = (
        P(None, ROW, COL),
        P(COL, None),
        P(None, ROW, None),
        P(ROW, COL),
        P(None, ROW, COL),
    )
    return jax.shard_map(shards, mesh=fine, in_specs=in_specs, out_specs=P(None, ROW, None), check_vma=False)
```

time: 271 us -> 204 us (0.75)
  blocking collectives: 164 us -> 119 us
  local copies, waits for them, and re-layouts: 31.8 us -> 2.08 us
  other arithmetic: 22.9 us -> 0 us
  starting transfers between devices: 11.1 us -> 32.8 us
  Pallas kernels: 0 us -> 19.5 us
  matrix products: 14.8 us -> 0 us
  waiting for transfers between devices: 23.6 us -> 29.8 us
    all_gather x3 -> x0, blocking collectives: 40.9 us -> none  [from_root(): lax.all_gather(array, axis)]
    all_to_all x2 -> x3, starting transfers between devices: 11.1 us -> 30.8 us  [exchanged(): return lax.all_to_all(parts, axes, split_axis=0, concat_axis=0, tiled=True)]
    unnamed x30 -> x4, local copies, waits for them, and re-layouts: 20.3 us -> 0.64 us
    pallas_call x0 -> x10, Pallas kernels: none -> 19.5 us  [the longest x3 11.9 us: factor(): pl.pallas_call(lambda *refs: factor_kernel(b, *refs), out_shape=jax.Shape...]
    all_to_all x8 -> x0, other arithmetic: 16.2 us -> none  [the longest x4 8.18 us: sum_at_owner(): lax.all_to_all(parts, axis, split_axis=0, concat_axis=0, tiled=True)]
    dot_general x4 -> x0, matrix products: 14.8 us -> none  [the longest x1 4.09 us: shards(): leading_part = jnp.dot(inverses[0], first_segment, precision=highest)]
    all_to_all x2 -> x3, waiting for transfers between devices: 23.6 us -> 29.8 us  [exchanged(): return lax.all_to_all(parts, axes, split_axis=0, concat_axis=0, tiled=True)]
    all_to_all x6, blocking collectives: 123 us -> 119 us  [exchanged(): return lax.all_to_all(parts, axes, split_axis=0, concat_axis=0, tiled=True)]
  transfers between devices with their start and end apart: 2 -> 6, of which waited for: 2 -> 3; matrix products, arithmetic and copies ran while one was open for 1% -> 0% of each run, Pallas kernels for 0% -> 2%
where the time goes in v1:
time: 204 us; the launch traced here: 203 us
  blocking collectives  119 us (58%)
  starting transfers between devices  32.8 us (16%)
  waiting for transfers between devices  29.8 us (15%)
  Pallas kernels  19.5 us (10%)
  local copies, waits for them, and re-layouts  2.08 us (1%)
    all_to_all x6, blocking collectives, exchanged(): return lax.all_to_all(parts, axes, split_axis=0, concat_axis=0, tiled=True)  119 us
    all_to_all x3, starting transfers between devices, exchanged(): return lax.all_to_all(parts, axes, split_axis=0, concat_axis=0, tiled=True)  30.8 us
    all_to_all x3, waiting for transfers between devices, exchanged(): return lax.all_to_all(parts, axes, split_axis=0, concat_axis=0, tiled=True)  29.8 us
    pallas_call x3, Pallas kernels, factor(): pl.pallas_call(lambda *refs: factor_kernel(b, *refs), out_shape=jax.Shape...  11.9 us
    pallas_call x2, Pallas kernels, carried(): pl.pallas_call(lambda *refs: carry_kernel(b, *refs), out_shape=jax.ShapeD...  6.54 us
  transfers between devices with their start and end apart: 6, of which 3 were waited for; matrix products, arithmetic and copies ran while one was open for 0% of the time, Pallas kernels for 2%

profile of v1, /device:TPU:8, one launch (start us, length us, event | category | flops | bytes accessed | tf_op | source)
XLA Modules:
  0.0 203.1 jit_solution(2614081832318055455)
XLA Ops:
  0.0 0.0 copy-start
  0.0 3.3 %carry0.1 = f32[32,24,128]{2,1,0:T(8,128)} custom-call(f32[64,192]{1,0:T(8,128)} %bitcast.22, f32[2,192,1536]{2,1,0:T(8,128)} %bitcast.19), custom_call_target="tpu_custom_call" | custom-call | tf_op jit(solution)/shard_map/carry0/pallas_call | solution.py:63
  3.3 11.7 %all-to-all-start = ((f32[32,24,128]{2,1,0:T(8,128)}), f32[32,24,128]{2,1,0:T(8,128)S(1)}, u32[]{:S(2)}, u32[]{:S(2)}) async-start(f32[32,24,128]{2,1,0:T(8,128)} %carry0.1), calls=%async_computation | async-start | bytes 786432 | tf_op jit(solution)/shard_map/all_to_all | solution.py:146
  15.0 0.0 copy-done
  15.1 14.0 %all-to-all-done.refs_0_ = f32[32,24,128]{2,1,0:T(8,128)S(1)} async-done(((f32[32,24,128]{2,1,0:T(8,128)}), f32[32,24,128]{2,1,0:T(8,128)S(1)}, u32[]{:S(2)}, u32[]{:S(2)}) %all-to-all-start) | async-done | bytes 393248 | tf_op jit(solution)/shard_map/all_to_all | solution.py:146
  29.1 0.7 collective-permute-start
  29.8 0.0 collective-permute-done
  29.8 21.2 %all_to_all.45.refs_0_ = f32[8,24,128]{2,1,0:T(8,128)} all-to-all(f32[8,24,128]{2,1,0:T(8,128)S(1)} %broadcast_in_dim.32), channel_id=1, replica_groups=mesh['z'=8,'y'=4,'x'=4,'c'=2] {'x','c'}, dimensions={0} | all-to-all | bytes 196608 | tf_op jit(solution)/shard_map/all_to_all | solution.py:146
  51.0 3.9 %factor.3 = f32[32,24,128]{2,1,0:T(8,128)} custom-call(f32[8,24,128]{2,1,0:T(8,128)} %all_to_all.45.refs_0_, f32[2,1536,384]{2,1,0:T(8,128)} %refs_1_.3), custom_call_target="tpu_custom_call" | custom-call | tf_op jit(solution)/shard_map/factor/pallas_call | solution.py:87
  54.9 19.3 %all_to_all.46.refs_0_ = f32[32,24,128]{2,1,0:T(8,128)S(1)} all-to-all(f32[32,24,128]{2,1,0:T(8,128)} %factor.3), channel_id=1, replica_groups=mesh['z'=8,'y'=4,'x'=4,'c'=2] {'z','y'}, dimensions={0} | all-to-all | bytes 786432 | tf_op jit(solution)/shard_map/all_to_all | solution.py:146
  74.2 0.7 collective-permute-start.1
  74.9 0.0 collective-permute-done.1
  74.9 0.6 broadcast_in_dim.36
  75.5 13.5 %all-to-all-start.4 = ((f32[8,24,128]{2,1,0:T(8,128)}), f32[8,24,128]{2,1,0:T(8,128)S(1)}, u32[]{:S(2)}, u32[]{:S(2)}) async-start(f32[8,24,128]{2,1,0:T(8,128)} %broadcast_in_dim.36), calls=%async_computation.4 | async-start | bytes 196608 | tf_op jit(solution)/shard_map/all_to_all | solution.py:146
  89.1 3.2 %carry1.1.refs_2_ = f32[32,24,128]{2,1,0:T(8,128)} custom-call(f32[64,192]{1,0:T(8,128)} %bitcast.23, f32[2,192,1536]{2,1,0:T(8,128)} %bitcast.20), custom_call_target="tpu_custom_call" | custom-call | tf_op jit(solution)/shard_map/carry1/pallas_call | solution.py:63
  92.3 2.6 %all-to-all-done.4.refs_0_ = f32[8,24,128]{2,1,0:T(8,128)S(1)} async-done(((f32[8,24,128]{2,1,0:T(8,128)}), f32[8,24,128]{2,1,0:T(8,128)S(1)}, u32[]{:S(2)}, u32[]{:S(2)}) %all-to-all-start.4) | async-done | bytes 98336 | tf_op jit(solution)/shard_map/all_to_all | solution.py:146
  94.9 0.0 copy-start.1
  94.9 0.6 copy-done.1
  95.5 4.1 %factor.4 = f32[32,24,128]{2,1,0:T(8,128)} custom-call(f32[8,24,128]{2,1,0:T(8,128)} %copy-done.1, f32[1,1536,384]{2,1,0:T(8,128)} %bitcast.21, f32[32,24,128]{2,1,0:T(8,128)} %carry1.1.refs_2_), custom_call_target="tpu_custom_call" | custom-call | tf_op jit(solution)/shard_map/factor/pallas_call | solution.py:87
  99.6 20.4 %all_to_all.47.refs_0_ = f32[32,24,128]{2,1,0:T(8,128)S(1)} all-to-all(f32[32,24,128]{2,1,0:T(8,128)} %factor.4), channel_id=1, replica_groups=mesh['z'=8,'y'=4,'x'=4,'c'=2] {'z','y'}, dimensions={0} | all-to-all | bytes 786432 | tf_op jit(solution)/shard_map/all_to_all | solution.py:146
  120.0 0.7 collective-permute-start.2
  120.7 0.0 collective-permute-done.2
  120.7 19.6 %all_to_all.48.refs_0_ = f32[8,24,128]{2,1,0:T(8,128)} all-to-all(f32[8,24,128]{2,1,0:T(8,128)S(1)} %broadcast_in_dim.39), channel_id=1, replica_groups=mesh['z'=8,'y'=4,'x'=4,'c'=2] {'x','c'}, dimensions={0} | all-to-all | bytes 196608 | tf_op jit(solution)/shard_map/all_to_all | solution.py:146
  140.3 3.9 %factor.5 = f32[32,24,128]{2,1,0:T(8,128)} custom-call(f32[8,24,128]{2,1,0:T(8,128)} %all_to_all.48.refs_0_, f32[2,1536,384]{2,1,0:T(8,128)} %refs_1_.3), custom_call_target="tpu_custom_call" | custom-call | tf_op jit(solution)/shard_map/factor/pallas_call | solution.py:87
  144.2 19.9 %all_to_all.49.refs_0_ = f32[32,24,128]{2,1,0:T(8,128)S(1)} all-to-all(f32[32,24,128]{2,1,0:T(8,128)} %factor.5), channel_id=1, replica_groups=mesh['z'=8,'y'=4,'x'=4,'c'=2] {'z','y'}, dimensions={0} | all-to-all | bytes 786432 | tf_op jit(solution)/shard_map/all_to_all | solution.py:146
  164.2 0.8 broadcast_in_dim.34
  164.9 5.6 %all-to-all-start.3 = ((f32[32,24,128]{2,1,0:T(8,128)}), f32[32,24,128]{2,1,0:T(8,128)S(1)}, u32[]{:S(2)}, u32[]{:S(2)}) async-start(f32[32,24,128]{2,1,0:T(8,128)} %broadcast_in_dim.34), calls=%async_computation.3 | async-start | bytes 786432 | tf_op jit(solution)/shard_map/all_to_all | solution.py:146
  170.6 13.2 %all-to-all-done.3.leading_ref = f32[32,24,128]{2,1,0:T(8,128)S(1)} async-done(((f32[32,24,128]{2,1,0:T(8,128)}), f32[32,24,128]{2,1,0:T(8,128)S(1)}, u32[]{:S(2)}, u32[]{:S(2)}) %all-to-all-start.3) | async-done | bytes 393248 | tf_op jit(solution)/shard_map/all_to_all | solution.py:146
  183.8 18.4 %all_to_all.50.trailing_ref = f32[32,24,128]{2,1,0:T(8,128)S(1)} all-to-all(f32[32,24,128]{2,1,0:T(8,128)S(1)} %total.7), channel_id=1, replica_groups=mesh['z'=8,'y'=4,'x'=4,'c'=2] {'z','y'}, dimensions={0} | all-to-all | bytes 786432 | tf_op jit(solution)/shard_map/all_to_all | solution.py:146
  202.2 0.9 finish.1
  (8 shorter events, 0.1 us)
Async XLA Ops:
  0.0 15.0 %copy-start = (f32[2,1536,64]{1,2,0:T(8,128)S(1)}, f32[2,1536,64]{1,2,0:T(8,128)}, u32[]{:S(2)}) copy-start(f32[2,1536,64]{1,2,0:T(8,128)} %param.7) | copy-start | bytes 2359300
  3.3 25.7 %all-to-all-start = ((f32[32,24,128]{2,1,0:T(8,128)}), f32[32,24,128]{2,1,0:T(8,128)S(1)}, u32[]{:S(2)}, u32[]{:S(2)}) async-start(f32[32,24,128]{2,1,0:T(8,128)} %carry0.1), calls=%async_computation | async-start | bytes 786432 | tf_op jit(solution)/shard_map/all_to_all | solution.py:146
  29.1 0.7 collective-permute-start
  74.2 0.7 collective-permute-start.1
  75.5 19.3 %all-to-all-start.4 = ((f32[8,24,128]{2,1,0:T(8,128)}), f32[8,24,128]{2,1,0:T(8,128)S(1)}, u32[]{:S(2)}, u32[]{:S(2)}) async-start(f32[8,24,128]{2,1,0:T(8,128)} %broadcast_in_dim.36), calls=%async_computation.4 | async-start | bytes 196608 | tf_op jit(solution)/shard_map/all_to_all | solution.py:146
  94.9 0.6 copy-start.1
  120.0 0.7 collective-permute-start.2
  164.9 18.9 %all-to-all-start.3 = ((f32[32,24,128]{2,1,0:T(8,128)}), f32[32,24,128]{2,1,0:T(8,128)S(1)}, u32[]{:S(2)}, u32[]{:S(2)}) async-start(f32[32,24,128]{2,1,0:T(8,128)} %broadcast_in_dim.34), calls=%async_computation.3 | async-start | bytes 786432 | tf_op jit(solution)/shard_map/all_to_all | solution.py:146

commit v2 on v1

--- a/solution.py
+++ b/solution.py
@@ -41,7 +41,7 @@
         for z in range(8):
             part = value[8 * z : 8 * z + 8, 128 * at : 128 * at + 128]
             if add_ref is not None:
-                part = part + add_ref[4 * z + y, 8 * t : 8 * t + 8, :]
+                part = add_ref[4 * z + y, 8 * t : 8 * t + 8, :] - part
             out_ref[4 * z + y, 8 * t : 8 * t + 8, :] = part
 
 
@@ -54,21 +54,30 @@
         yield g
 
 
-def carry_kernel(b, prior_ref, panel_ref, out_ref, buffer, sems):
+def carry_kernel(b, first_ref, prior_ref, panel_ref, right_ref, out_ref, buffer, sems):
     for g in chunks(lambda g: panel_ref.at[b, :, pl.ds(512 * g, 512)], buffer, sems):
-        put_slots(out_ref, product(prior_ref[...], buffer[g], 0), 512 * g)
-
-
-def carried(prior_t, panel_t, b):
+        put_slots(out_ref, -product(prior_ref[...], buffer[g], 0), 512 * g)
+
+    @pl.when(first_ref[0] == 1)
+    def _():
+        for z in range(8):
+            for y in range(4):
+                for t in range(3):
+                    rows = slice(8 * t, 8 * t + 8)
+                    lanes = 384 * y + 128 * t
+                    out_ref[4 * z + y, rows, :] += right_ref[b, 8 * z : 8 * z + 8, lanes : lanes + 128]
+
+
+def carried(first, prior_t, panel_t, right_t, b):
     return pl.pallas_call(
         lambda *refs: carry_kernel(b, *refs),
         out_shape=jax.ShapeDtypeStruct((32, *SLOT), jnp.float32),
-        in_specs=[VMEM, HBM],
+        in_specs=[pl.BlockSpec(memory_space=pltpu.SMEM), VMEM, HBM, VMEM],
         out_specs=VMEM,
         scratch_shapes=[pltpu.VMEM((3, 192, 512), jnp.float32), pltpu.SemaphoreType.DMA((3,))],
         compiler_params=grant(62),
         name=f"carry{b}",
-    )(prior_t, panel_t)
+    )(first, prior_t, panel_t, right_t)
 
 
 def joined(gathered_ref):
@@ -96,50 +105,50 @@
 
 
 def total_kernel(copies, parts_ref, *refs):
-    out_ref = refs[-1]
+    *with_ref, out_ref = refs
+    at = 24 * len(with_ref)
     for t in range(3):
         rows = slice(8 * t, 8 * t + 8)
         sums = [parts_ref[k, rows, :] for k in range(4)]
         for s in range(4, 32):
             sums[s % 4] = sums[s % 4] + parts_ref[s, rows, :]
         value = (sums[0] + sums[1]) + (sums[2] + sums[3])
-        if len(refs) > 1:
-            value = refs[0][rows, :] - value
         for k in range(copies):
-            out_ref[k, rows, :] = value
-
-
-def total(parts, copies, base=None):
-    args = [parts] if base is None else [parts, base]
+            for ref in with_ref:
+                out_ref[k, rows, :] = ref[rows, :]
+            out_ref[k, at + 8 * t : at + 8 * t + 8, :] = value
+
+
+def total(parts, copies, *beside):
     return pl.pallas_call(
         lambda *refs: total_kernel(copies, *refs),
-        out_shape=jax.ShapeDtypeStruct((copies, *SLOT), jnp.float32),
-        in_specs=[VMEM] * len(args),
+        out_shape=jax.ShapeDtypeStruct((copies, 24 + 24 * len(beside), 128), jnp.float32),
+        in_specs=[VMEM] * (1 + len(beside)),
         out_specs=VMEM,
         compiler_params=grant(4),
         name="total",
-    )(*args)
-
-
-def finish_kernel(leading_ref, trailing_ref, out_ref):
-    for b, ref in enumerate((leading_ref, trailing_ref)):
+    )(parts, *beside)
+
+
+def finish_kernel(gathered_ref, out_ref):
+    for b in range(2):
         for z in range(8):
             for y in range(4):
                 for t in range(3):
-                    out_ref[b, 8 * z : 8 * z + 8, 384 * y + 128 * t : 384 * y + 128 * t + 128] = ref[
-                        4 * z + y, 8 * t : 8 * t + 8, :
-                    ]
-
-
-def finish(leading, trailing):
+                    lanes = 384 * y + 128 * t
+                    rows = 24 * b + 8 * t
+                    out_ref[b, 8 * z : 8 * z + 8, lanes : lanes + 128] = gathered_ref[4 * z + y, rows : rows + 8, :]
+
+
+def finish(gathered):
     return pl.pallas_call(
         finish_kernel,
         out_shape=jax.ShapeDtypeStruct((2, 64, 1536), jnp.float32),
-        in_specs=[VMEM] * 2,
+        in_specs=[VMEM],
         out_specs=VMEM,
         compiler_params=grant(8),
         name="finish",
-    )(leading, trailing)
+    )(gathered)
 
 
 def exchanged(parts, axes):
@@ -153,30 +162,30 @@
 TURN = [(device(z, y, row), device(row, y, z)) for z in range(8) for y in range(4) for row in range(8)]
 
 
-def spread(piece):
-    turned = lax.ppermute(piece, ALL, TURN)
-    return exchanged(jnp.broadcast_to(turned, (8, *SLOT)), ROW)
+def dealt(parts):
+    return exchanged(parts.reshape(8, 96, 128), ROW).reshape(32, *SLOT)
 
 
 def shards(panel, prior, right_side, coupling, inverses):
     panel_t = panel.transpose(0, 2, 1)
     prior_t = prior.T
     right_t = right_side.transpose(0, 2, 1)
-    z, y = lax.axis_index("z"), lax.axis_index("y")
-    own = lax.dynamic_slice(right_t, (0, 8 * z, 384 * y), (2, 8, 384))
-    own = own.reshape(2, 8, 3, 128).transpose(0, 2, 1, 3).reshape(2, *SLOT)
-
-    first = total(exchanged(carried(prior_t, panel_t, 0), COL), 1, own[0])
-    later = carried(prior_t, panel_t, 1)
-    leading_parts = factor(spread(first), inverses, 0)
-    leading = total(exchanged(leading_parts, COL), 1)
-    second_parts = factor(spread(leading), coupling[None], 0, later)
-    second = total(exchanged(second_parts, COL), 1, own[1])
-    leading_all = exchanged(jnp.broadcast_to(leading, (32, *SLOT)), COL)
-    trailing_parts = factor(spread(second), inverses, 1)
-    trailing = total(exchanged(trailing_parts, COL), 32)
-    trailing_all = exchanged(trailing, COL)
-    return finish(leading_all, trailing_all).transpose(0, 2, 1)
+    column = lax.axis_index("z") * 4 + lax.axis_index("y")
+    first_column = (column == 0).astype(jnp.int32).reshape(1)
+
+    first_parts = carried(first_column, prior_t, panel_t, right_t, 0)
+    later = carried(first_column, prior_t, panel_t, right_t, 1)
+    first = exchanged(total(exchanged(dealt(first_parts), COL), 8), ROW)
+    first, later = lax.optimization_barrier((first, later))
+    leading_parts = factor(first, inverses, 0)
+    leading = total(exchanged(dealt(leading_parts), COL), 8)
+    second_parts = factor(exchanged(leading, ROW), coupling[None], 0, later)
+    second_dealt, piece = lax.optimization_barrier((dealt(second_parts), leading[0]))
+    arrived, piece = lax.optimization_barrier((exchanged(second_dealt, COL), lax.ppermute(piece, ALL, TURN)))
+    second = exchanged(total(arrived, 8), ROW)
+    trailing_parts = factor(second, inverses, 1)
+    both = total(exchanged(trailing_parts, COL), 32, piece)
+    return finish(exchanged(both, COL)).transpose(0, 2, 1)
 
 
 def solution(mesh):

time: 204 us -> 197 us (0.966)
  starting transfers between devices: 32.8 us -> 13.7 us
  blocking collectives: 119 us -> 137 us
  waiting for transfers between devices: 29.8 us -> 23.8 us
    all_to_all x6 -> x8, blocking collectives: 119 us -> 137 us  [exchanged(): return lax.all_to_all(parts, axes, split_axis=0, concat_axis=0, tiled=True)]
    all_to_all x3, starting transfers between devices: 30.8 us -> 13 us  [exchanged(): return lax.all_to_all(parts, axes, split_axis=0, concat_axis=0, tiled=True)]
    all_to_all x3, waiting for transfers between devices: 29.8 us -> 23.8 us  [exchanged(): return lax.all_to_all(parts, axes, split_axis=0, concat_axis=0, tiled=True)]
  transfers between devices with their start and end apart: 6 -> 4, of which waited for: 3 -> 3; matrix products, arithmetic and copies ran while one was open for 0% -> 0% of each run, Pallas kernels for 2% -> 2%
where the time goes in v2:
time: 197 us; the launch traced here: 196 us
  blocking collectives  137 us (70%)
  waiting for transfers between devices  23.8 us (12%)
  Pallas kernels  20.7 us (11%)
  starting transfers between devices  13.7 us (7%)
    all_to_all x8, blocking collectives, exchanged(): return lax.all_to_all(parts, axes, split_axis=0, concat_axis=0, tiled=True)  137 us
    all_to_all x3, waiting for transfers between devices, exchanged(): return lax.all_to_all(parts, axes, split_axis=0, concat_axis=0, tiled=True)  23.8 us
    all_to_all x3, starting transfers between devices, exchanged(): return lax.all_to_all(parts, axes, split_axis=0, concat_axis=0, tiled=True)  13 us
    pallas_call x3, Pallas kernels, factor(): pl.pallas_call(lambda *refs: factor_kernel(b, *refs), out_shape=jax.Shape...  11.9 us
    pallas_call x2, Pallas kernels, carried(): pl.pallas_call(lambda *refs: carry_kernel(b, *refs), out_shape=jax.ShapeD...  7.14 us
  transfers between devices with their start and end apart: 4, of which 3 were waited for; matrix products, arithmetic and copies ran while one was open for 0% of the time, Pallas kernels for 2%

profile of v2, /device:TPU:8, one launch (start us, length us, event | category | flops | bytes accessed | tf_op | source)
XLA Modules:
  0.0 195.9 jit_solution(15104539993660096295)
XLA Ops:
  0.0 3.6 %carry0.1 = f32[32,24,128]{2,1,0:T(8,128)} custom-call(s32[1]{0:T(128)} %bitcast.refs_0_, f32[64,192]{1,0:T(8,128)} %bitcast.24, f32[2,192,1536]{2,1,0:T(8,128)} %bitcast.14, f32[2,64,1536]{2,1,0:T(8,128)} %bitcast.16), custom_call_target="tpu_custom_call" | custom-call | tf_op jit(solution)/shard_map/carry0/pallas_call | solution.py:72
  3.6 13.2 %all_to_all.55 = f32[8,96,128]{2,1,0:T(8,128)S(1)} all-to-all(f32[8,96,128]{2,1,0:T(8,128)} %bitcast.23), channel_id=1, replica_groups=mesh['z'=8,'y'=4,'x'=4,'c'=2] {'x','c'}, dimensions={0} | all-to-all | bytes 786432 | tf_op jit(solution)/shard_map/all_to_all | solution.py:155
  16.8 25.3 %all_to_all.56.refs_0_ = f32[32,24,128]{2,1,0:T(8,128)S(1)} all-to-all(f32[32,24,128]{2,1,0:T(8,128)S(1)} %bitcast.20), channel_id=1, replica_groups=mesh['z'=8,'y'=4,'x'=4,'c'=2] {'z','y'}, dimensions={0} | all-to-all | bytes 786432 | tf_op jit(solution)/shard_map/all_to_all | solution.py:155
  42.1 0.7 total.4
  42.8 3.4 %all-to-all-start.2 = ((f32[8,24,128]{2,1,0:T(8,128)}), f32[8,24,128]{2,1,0:T(8,128)S(1)}, u32[]{:S(2)}, u32[]{:S(2)}) async-start(f32[8,24,128]{2,1,0:T(8,128)} %total.4), calls=%async_computation.2 | async-start | bytes 196608 | tf_op jit(solution)/shard_map/all_to_all | solution.py:155
  46.2 3.6 %carry1.1.refs_2_ = f32[32,24,128]{2,1,0:T(8,128)} custom-call(s32[1]{0:T(128)} %bitcast.refs_0_, f32[64,192]{1,0:T(8,128)} %bitcast.25, f32[2,192,1536]{2,1,0:T(8,128)} %bitcast.15, f32[2,64,1536]{2,1,0:T(8,128)} %bitcast.17), custom_call_target="tpu_custom_call" | custom-call | tf_op jit(solution)/shard_map/carry1/pallas_call | solution.py:72
  49.7 2.1 %all-to-all-done.2.refs_0_ = f32[8,24,128]{2,1,0:T(8,128)S(1)} async-done(((f32[8,24,128]{2,1,0:T(8,128)}), f32[8,24,128]{2,1,0:T(8,128)S(1)}, u32[]{:S(2)}, u32[]{:S(2)}) %all-to-all-start.2) | async-done | bytes 98336 | tf_op jit(solution)/shard_map/all_to_all | solution.py:155
  51.9 0.0 copy-start
  51.9 0.6 copy-done
  52.5 3.9 %factor.3 = f32[32,24,128]{2,1,0:T(8,128)} custom-call(f32[8,24,128]{2,1,0:T(8,128)} %copy-done, f32[2,1536,384]{2,1,0:T(8,128)} %refs_1_.3), custom_call_target="tpu_custom_call" | custom-call | tf_op jit(solution)/shard_map/factor/pallas_call | solution.py:96
  56.4 12.3 %all_to_all.57 = f32[8,96,128]{2,1,0:T(8,128)S(1)} all-to-all(f32[8,96,128]{2,1,0:T(8,128)} %bitcast.21), channel_id=1, replica_groups=mesh['z'=8,'y'=4,'x'=4,'c'=2] {'x','c'}, dimensions={0} | all-to-all | bytes 786432 | tf_op jit(solution)/shard_map/all_to_all | solution.py:155
  68.7 19.2 %all_to_all.58.refs_0_ = f32[32,24,128]{2,1,0:T(8,128)S(1)} all-to-all(f32[32,24,128]{2,1,0:T(8,128)S(1)} %bitcast.22), channel_id=1, replica_groups=mesh['z'=8,'y'=4,'x'=4,'c'=2] {'z','y'}, dimensions={0} | all-to-all | bytes 786432 | tf_op jit(solution)/shard_map/all_to_all | solution.py:155
  87.9 8.9 %all_to_all.59.refs_0_ = f32[8,24,128]{2,1,0:T(8,128)} all-to-all(f32[8,24,128]{2,1,0:T(8,128)S(1)} %total.5), channel_id=1, replica_groups=mesh['z'=8,'y'=4,'x'=4,'c'=2] {'x','c'}, dimensions={0} | all-to-all | bytes 196608 | tf_op jit(solution)/shard_map/all_to_all | solution.py:155
  96.8 4.1 %factor.4 = f32[32,24,128]{2,1,0:T(8,128)} custom-call(f32[8,24,128]{2,1,0:T(8,128)} %all_to_all.59.refs_0_, f32[1,1536,384]{2,1,0:T(8,128)} %bitcast.18, f32[32,24,128]{2,1,0:T(8,128)} %carry1.1.refs_2_), custom_call_target="tpu_custom_call" | custom-call | tf_op jit(solution)/shard_map/factor/pallas_call | solution.py:96
  100.8 4.1 %all-to-all-start.6 = ((f32[8,96,128]{2,1,0:T(8,128)}), f32[8,96,128]{2,1,0:T(8,128)}, u32[]{:S(2)}, u32[]{:S(2)}) async-start(f32[8,96,128]{2,1,0:T(8,128)} %bitcast.19), calls=%async_computation.6 | async-start | bytes 786432 | tf_op jit(solution)/shard_map/all_to_all | solution.py:155
  105.0 8.9 %all-to-all-done.6 = f32[8,96,128]{2,1,0:T(8,128)} async-done(((f32[8,96,128]{2,1,0:T(8,128)}), f32[8,96,128]{2,1,0:T(8,128)}, u32[]{:S(2)}, u32[]{:S(2)}) %all-to-all-start.6) | async-done | bytes 393248 | tf_op jit(solution)/shard_map/all_to_all | solution.py:155
  113.9 5.6 %all-to-all-start.7 = ((f32[32,24,128]{2,1,0:T(8,128)}), f32[32,24,128]{2,1,0:T(8,128)S(1)}, u32[]{:S(2)}, u32[]{:S(2)}) async-start(f32[32,24,128]{2,1,0:T(8,128)} %bitcast.10), calls=%async_computation.7 | async-start | bytes 786432 | tf_op jit(solution)/shard_map/all_to_all | solution.py:155
  119.4 0.7 collective-permute-start
  120.1 0.0 collective-permute-done.refs_1_
  120.1 12.8 %all-to-all-done.7.refs_0_ = f32[32,24,128]{2,1,0:T(8,128)S(1)} async-done(((f32[32,24,128]{2,1,0:T(8,128)}), f32[32,24,128]{2,1,0:T(8,128)S(1)}, u32[]{:S(2)}, u32[]{:S(2)}) %all-to-all-start.7) | async-done | bytes 393248 | tf_op jit(solution)/shard_map/all_to_all | solution.py:155
  133.0 10.1 %all_to_all.60.refs_0_ = f32[8,24,128]{2,1,0:T(8,128)} all-to-all(f32[8,24,128]{2,1,0:T(8,128)S(1)} %total.6), channel_id=1, replica_groups=mesh['z'=8,'y'=4,'x'=4,'c'=2] {'x','c'}, dimensions={0} | all-to-all | bytes 196608 | tf_op jit(solution)/shard_map/all_to_all | solution.py:155
  143.0 3.9 %factor.5 = f32[32,24,128]{2,1,0:T(8,128)} custom-call(f32[8,24,128]{2,1,0:T(8,128)} %all_to_all.60.refs_0_, f32[2,1536,384]{2,1,0:T(8,128)} %refs_1_.3), custom_call_target="tpu_custom_call" | custom-call | tf_op jit(solution)/shard_map/factor/pallas_call | solution.py:96
  147.0 20.9 %all_to_all.61.refs_0_ = f32[32,24,128]{2,1,0:T(8,128)S(1)} all-to-all(f32[32,24,128]{2,1,0:T(8,128)} %factor.5), channel_id=1, replica_groups=mesh['z'=8,'y'=4,'x'=4,'c'=2] {'z','y'}, dimensions={0} | all-to-all | bytes 786432 | tf_op jit(solution)/shard_map/all_to_all | solution.py:155
  167.8 0.1 total.7
  167.9 27.1 %all_to_all.62.gathered_ref = f32[32,48,128]{2,1,0:T(8,128)S(1)} all-to-all(f32[32,48,128]{2,1,0:T(8,128)S(1)} %total.7), channel_id=1, replica_groups=mesh['z'=8,'y'=4,'x'=4,'c'=2] {'z','y'}, dimensions={0} | all-to-all | bytes 1572864 | tf_op jit(solution)/shard_map/all_to_all | solution.py:155
  195.0 0.9 finish.1
  (3 shorter events, 0.1 us)
Async XLA Ops:
  42.8 9.1 %all-to-all-start.2 = ((f32[8,24,128]{2,1,0:T(8,128)}), f32[8,24,128]{2,1,0:T(8,128)S(1)}, u32[]{:S(2)}, u32[]{:S(2)}) async-start(f32[8,24,128]{2,1,0:T(8,128)} %total.4), calls=%async_computation.2 | async-start | bytes 196608 | tf_op jit(solution)/shard_map/all_to_all | solution.py:155
  51.9 0.6 copy-start
  100.8 13.0 %all-to-all-start.6 = ((f32[8,96,128]{2,1,0:T(8,128)}), f32[8,96,128]{2,1,0:T(8,128)}, u32[]{:S(2)}, u32[]{:S(2)}) async-start(f32[8,96,128]{2,1,0:T(8,128)} %bitcast.19), calls=%async_computation.6 | async-start | bytes 786432 | tf_op jit(solution)/shard_map/all_to_all | solution.py:155
  113.9 19.1 %all-to-all-start.7 = ((f32[32,24,128]{2,1,0:T(8,128)}), f32[32,24,128]{2,1,0:T(8,128)S(1)}, u32[]{:S(2)}, u32[]{:S(2)}) async-start(f32[32,24,128]{2,1,0:T(8,128)} %bitcast.10), calls=%async_computation.7 | async-start | bytes 786432 | tf_op jit(solution)/shard_map/all_to_all | solution.py:155
  119.4 0.7 collective-permute-start

commit v3 on v2

v3 whole, which is shorter than its diff:
```python
import jax
import jax.numpy as jnp
from jax import lax
from jax.experimental import pallas as pl
from jax.experimental.pallas import tpu as pltpu
from jax.sharding import Mesh, PartitionSpec as P

ROW = ("x", "c")
COL = ("z", "y")
ALL = ("z", "y", "x", "c")
DEAL = ("y", "x", "c")
SLOT = (24, 128)
VMEM = pl.BlockSpec(memory_space=pltpu.VMEM)
SMEM = pl.BlockSpec(memory_space=pltpu.SMEM)
HBM = pl.BlockSpec(memory_space=pltpu.HBM)


def grant(mib):
    return pltpu.CompilerParams(vmem_limit_bytes=mib << 20)


def array(*shape, dtype=jnp.float32):
    return jax.ShapeDtypeStruct(shape, dtype)


def halves(value):
    high = value.astype(jnp.bfloat16)
    low = (value - high.astype(jnp.float32)).astype(jnp.bfloat16)
    return high, low


def product(left, right_high, right_low, contract):
    left_high, left_low = halves(left)
    dims = (((1,), (contract,)), ((), ()))
    both = lax.dot_general(
        jnp.concatenate([left_high, left_low], 0), right_high, dims, preferred_element_type=jnp.float32
    )
    rest = lax.dot_general(left_high, right_low, dims, preferred_element_type=jnp.float32)
    return both[:64] + (both[64:] + rest)


def dealt_slot(z, y):
    return 8 * y + z


def column_slot(z, y):
    return 4 * z + y


def put_slots(slot, out_ref, value, start, add_ref=None):
    for at in range(value.shape[1] // 128):
        tile = start // 128 + at
        y, rows = tile // 3, slice(tile % 3 * 8, tile % 3 * 8 + 8)
        for z in range(8):
            part = value[8 * z : 8 * z + 8, 128 * at : 128 * at + 128]
            if add_ref is not None:
                part = add_ref[slot(z, y), rows, :] - part
            out_ref[slot(z, y), rows, :] = part


def carry_kernel(b, place_ref, prior_ref, panel_ref, right_ref, out_ref, buffer, piece, sems):
    z, y = place_ref[0], place_ref[1]
    copies = [
        pltpu.make_async_copy(panel_ref.at[b, :, pl.ds(512 * g, 512)], buffer.at[g], sems.at[g]) for g in range(3)
    ]
    copies.append(
        pltpu.make_async_copy(
            right_ref.at[b, pl.ds(pl.multiple_of(8 * z, 8), 8), pl.ds(pl.multiple_of(384 * y, 128), 384)],
            piece,
            sems.at[3],
        )
    )
    for copy in copies:
        copy.start()
    for g in range(3):
        copies[g].wait()
        put_slots(dealt_slot, out_ref, -product(prior_ref[...], *halves(buffer[g]), 0), 512 * g)
    copies[3].wait()
    own = dealt_slot(z, y)
    for t in range(3):
        out_ref[pl.ds(own, 1), 8 * t : 8 * t + 8, :] += piece[:, 128 * t : 128 * t + 128][None]


def carried(place, prior_t, panel_t, right_t, b):
    return pl.pallas_call(
        lambda *refs: carry_kernel(b, *refs),
        out_shape=array(32, *SLOT),
        in_specs=[SMEM, VMEM, HBM, HBM],
        out_specs=VMEM,
        scratch_shapes=[
            pltpu.VMEM((3, 192, 512), jnp.float32),
            pltpu.VMEM((8, 384), jnp.float32),
            pltpu.SemaphoreType.DMA((4,)),
        ],
        compiler_params=grant(62),
        name=f"carry{b}",
    )(place, prior_t, panel_t, right_t)


def split_kernel(matrix_ref, high_ref, low_ref):
    for start in range(0, 1536, 128):
        rows = slice(start, start + 128)
        high_ref[rows, :], low_ref[rows, :] = halves(matrix_ref[rows, :])


def split(matrix):
    return pl.pallas_call(
        split_kernel,
        out_shape=[array(1536, 384, dtype=jnp.bfloat16)] * 2,
        in_specs=[VMEM],
        out_specs=[VMEM] * 2,
        compiler_params=grant(4),
        name="split",
    )(matrix)


def joined(gathered_ref):
    return jnp.concatenate(
        [jnp.concatenate([gathered_ref[e, 8 * t : 8 * t + 8, :] for t in range(3)], 1) for e in range(8)], 0
    )


def factor_kernel(slot, gathered_ref, high_ref, low_ref, *refs):
    *add, out_ref = refs
    vector = joined(gathered_ref)
    for start in range(0, 1536, 512):
        rows = slice(start, start + 512)
        put_slots(slot, out_ref, product(vector, high_ref[rows, :], low_ref[rows, :], 1), start, *add)


def factor(slot, gathered, matrix, *add):
    return pl.pallas_call(
        lambda *refs: factor_kernel(slot, *refs),
        out_shape=array(32, *SLOT),
        in_specs=[VMEM] * (3 + len(add)),
        out_specs=VMEM,
        compiler_params=grant(8),
        name="factor",
    )(gathered, *matrix, *add)


def sum_of(values):
    values = list(values)
    while len(values) > 1:
        values = [a + b for a, b in zip(values[::2], values[1::2])]
    return values[0]


def fold_kernel(parts_ref, out_ref):
    for a in range(8):
        out_ref[a] = sum_of(parts_ref[8 * y + a] for y in range(4))


def fold(parts):
    return pl.pallas_call(
        fold_kernel,
        out_shape=array(8, *SLOT),
        in_specs=[VMEM],
        out_specs=VMEM,
        compiler_params=grant(4),
        name="fold",
    )(parts)


def total_kernel(copies, parts_ref, *refs):
    *with_ref, out_ref = refs
    at = 24 * len(with_ref)
    for t in range(3):
        rows = slice(8 * t, 8 * t + 8)
        value = sum_of(parts_ref[s, rows, :] for s in range(parts_ref.shape[0]))
        for k in range(copies):
            for ref in with_ref:
                out_ref[k, rows, :] = ref[rows, :]
            out_ref[k, at + 8 * t : at + 8 * t + 8, :] = value


def total(parts, copies, *beside):
    return pl.pallas_call(
        lambda *refs: total_kernel(copies, *refs),
        out_shape=array(copies, 24 + 24 * len(beside), 128),
        in_specs=[VMEM] * (1 + len(beside)),
        out_specs=VMEM,
        compiler_params=grant(4),
        name="total",
    )(parts, *beside)


def finish_kernel(gathered_ref, out_ref):
    for b in range(2):
        for z in range(8):
            for y in range(4):
                for t in range(3):
                    lanes = 384 * y + 128 * t
                    rows = 24 * b + 8 * t
                    out_ref[b, 8 * z : 8 * z + 8, lanes : lanes + 128] = gathered_ref[
                        column_slot(z, y), rows : rows + 8, :
                    ]


def finish(gathered):
    return pl.pallas_call(
        finish_kernel,
        out_shape=array(2, 64, 1536),
        in_specs=[VMEM],
        out_specs=VMEM,
        compiler_params=grant(8),
        name="finish",
    )(gathered)


def exchanged(parts, axes):
    return lax.all_to_all(parts, axes, split_axis=0, concat_axis=0, tiled=True)


def device(z, y, row):
    return (z * 4 + y) * 8 + row


TURN = [(device(z, y, row), device(row, y, z)) for z in range(8) for y in range(4) for row in range(8)]


def during(parts, axes, work, *operands):
    parts, operands = lax.optimization_barrier((parts, operands))
    return exchanged(parts, axes), work(*operands)


def shards(panel, prior, right_side, coupling, inverses):
    panel_t = panel.transpose(0, 2, 1)
    prior_t = prior.T
    right_t = right_side.transpose(0, 2, 1)
    place = jnp.stack([lax.axis_index("z"), lax.axis_index("y")]).astype(jnp.int32)

    def second_carry(panel_t):
        return carried(place, prior_t, panel_t, right_t, 1)

    first_parts = carried(place, prior_t, panel_t, right_t, 0)
    moved, later = during(first_parts, DEAL, second_carry, panel_t)
    moved = exchanged(fold(moved), "z")
    first, matrix = during(total(moved, 8), ROW, lambda m: split(m[0]), inverses)
    moved = exchanged(factor(dealt_slot, first, matrix), DEAL)
    leading = total(exchanged(fold(moved), "z"), 8)
    gathered, matrix = during(leading, ROW, split, coupling)
    second_parts = factor(dealt_slot, gathered, matrix, later)
    moved, piece = during(second_parts, DEAL, lambda p: lax.ppermute(p, ALL, TURN), leading[0])
    moved = exchanged(fold(moved), "z")
    second, matrix = during(total(moved, 8), ROW, lambda m: split(m[1]), inverses)
    trailing_parts = factor(column_slot, second, matrix)
    both = total(exchanged(trailing_parts, COL), 32, piece)
    return finish(exchanged(both, COL)).transpose(0, 2, 1)


def solution(mesh):
    fine = Mesh(mesh.devices.reshape(8, 4, 4, 2), ALL)
    in_specs = (
        P(None, ROW, COL),
        P(COL, None),
        P(None, ROW, None),
        P(ROW, COL),
        P(None, ROW, COL),
    )
    return jax.shard_map(shards, mesh=fine, in_specs=in_specs, out_specs=P(None, ROW, None), check_vma=False)
```

time: 197 us -> 171 us (0.87)
  blocking collectives: 137 us -> 100 us
  Pallas kernels: 20.7 us -> 14.5 us
  waiting for transfers between devices: 23.8 us -> 29.6 us
  local copies, waits for them, and re-layouts: 0.64 us -> 6.02 us
  starting transfers between devices: 13.7 us -> 19 us
    all_to_all x8 -> x6, blocking collectives: 137 us -> 100 us  [exchanged(): return lax.all_to_all(parts, axes, split_axis=0, concat_axis=0, tiled=True)]
    pallas_call x10 -> x16, Pallas kernels: 20.7 us -> 14.5 us  [the longest x2 6.51 us: carried(): pl.pallas_call(lambda *refs: carry_kernel(b, *refs), out_shape=array(32,...]
    all_to_all x3 -> x5, waiting for transfers between devices: 23.8 us -> 29.6 us  [exchanged(): return lax.all_to_all(parts, axes, split_axis=0, concat_axis=0, tiled=True)]
    all_to_all x3 -> x5, starting transfers between devices: 13 us -> 18.4 us  [exchanged(): return lax.all_to_all(parts, axes, split_axis=0, concat_axis=0, tiled=True)]
    squeeze x0 -> x2, local copies, waits for them, and re-layouts: none -> 3.64 us  [the longest x1 1.82 us: shards(): m[1]]
  transfers between devices with their start and end apart: 4 -> 6, of which waited for: 3 -> 5; matrix products, arithmetic and copies ran while one was open for 0% -> 3% of each run, Pallas kernels for 2% -> 3%
where the time goes in v3:
time: 171 us; the launch traced here: 170 us
  blocking collectives  100 us (58%)
  waiting for transfers between devices  29.6 us (17%)
  starting transfers between devices  19 us (11%)
  Pallas kernels  14.5 us (8%)
  local copies, waits for them, and re-layouts  6.02 us (4%)
    all_to_all x6, blocking collectives, exchanged(): return lax.all_to_all(parts, axes, split_axis=0, concat_axis=0, tiled=True)  100 us
    all_to_all x5, waiting for transfers between devices, exchanged(): return lax.all_to_all(parts, axes, split_axis=0, concat_axis=0, tiled=True)  29.6 us
    all_to_all x5, starting transfers between devices, exchanged(): return lax.all_to_all(parts, axes, split_axis=0, concat_axis=0, tiled=True)  18.4 us
    pallas_call x2, Pallas kernels, carried(): pl.pallas_call(lambda *refs: carry_kernel(b, *refs), out_shape=array(32,...  6.51 us
  transfers between devices with their start and end apart: 6, of which 5 were waited for; matrix products, arithmetic and copies ran while one was open for 3% of the time, Pallas kernels for 3%

profile of v3, /device:TPU:8, one launch (start us, length us, event | category | flops | bytes accessed | tf_op | source)
XLA Modules:
  0.0 170.0 jit_solution(690883363352785640)
XLA Ops:
  0.0 0.6 pad_add_fusion.refs_0_
  0.6 3.3 %carry0.1 = f32[32,24,128]{2,1,0:T(8,128)} custom-call(s32[2]{0:T(128)} %pad_add_fusion.refs_0_, f32[64,192]{1,0:T(8,128)} %bitcast.16, f32[2,192,1536]{2,1,0:T(8,128)} %bitcast.12, f32[2,64,1536]{2,1,0:T(8,128)} %bitcast.14), custom_call_target="tpu_custom_call" | custom-call | tf_op jit(solution)/shard_map/carry0/pallas_call | solution.py:85
  3.9 16.2 %all_to_all.55.parts_ref = f32[32,24,128]{2,1,0:T(8,128)S(1)} all-to-all(f32[32,24,128]{2,1,0:T(8,128)} %carry0.1), channel_id=1, replica_groups=mesh['z'=8,'y'=4,'x'=4,'c'=2] {'y','x','c'}, dimensions={0} | all-to-all | bytes 786432 | tf_op jit(solution)/shard_map/all_to_all | solution.py:212
  20.0 17.4 %all_to_all.56.refs_0_ = f32[8,24,128]{2,1,0:T(8,128)S(1)} all-to-all(f32[8,24,128]{2,1,0:T(8,128)S(1)} %fold.3), channel_id=1, replica_groups=mesh['z'=8,'y'=4,'x'=4,'c'=2] {'z'}, dimensions={0} | all-to-all | bytes 196608 | tf_op jit(solution)/shard_map/all_to_all | solution.py:212
  37.5 0.7 total.4
  38.1 3.4 %all-to-all-start.2 = ((f32[8,24,128]{2,1,0:T(8,128)}), f32[8,24,128]{2,1,0:T(8,128)S(1)}, u32[]{:S(2)}, u32[]{:S(2)}) async-start(f32[8,24,128]{2,1,0:T(8,128)} %total.4), calls=%async_computation.2 | async-start | bytes 196608 | tf_op jit(solution)/shard_map/all_to_all | solution.py:212
  41.5 1.8 %slice_bitcast_fusion.1.matrix_ref = f32[1536,384]{1,0:T(8,128)S(1)} fusion(f32[2,1536,384]{2,1,0:T(8,128)} %param.9), kind=kLoop, calls=%fused_computation.1 | loop fusion | bytes 4718592 | tf_op jit(solution)/shard_map/squeeze | solution.py:239
  43.3 0.4 split.3
  43.7 3.5 %all-to-all-done.2.refs_0_ = f32[8,24,128]{2,1,0:T(8,128)S(1)} async-done(((f32[8,24,128]{2,1,0:T(8,128)}), f32[8,24,128]{2,1,0:T(8,128)S(1)}, u32[]{:S(2)}, u32[]{:S(2)}) %all-to-all-start.2) | async-done | bytes 98336 | tf_op jit(solution)/shard_map/all_to_all | solution.py:212
  47.2 0.8 factor.3
  48.1 13.3 %all_to_all.57.parts_ref = f32[32,24,128]{2,1,0:T(8,128)S(1)} all-to-all(f32[32,24,128]{2,1,0:T(8,128)S(1)} %factor.3), channel_id=1, replica_groups=mesh['z'=8,'y'=4,'x'=4,'c'=2] {'y','x','c'}, dimensions={0} | all-to-all | bytes 786432 | tf_op jit(solution)/shard_map/all_to_all | solution.py:212
  61.4 0.7 fold.4
  62.0 3.4 %all-to-all-start.4 = ((f32[8,24,128]{2,1,0:T(8,128)}), f32[8,24,128]{2,1,0:T(8,128)S(1)}, u32[]{:S(2)}, u32[]{:S(2)}) async-start(f32[8,24,128]{2,1,0:T(8,128)} %fold.4), calls=%async_computation.4 | async-start | bytes 196608 | tf_op jit(solution)/shard_map/all_to_all | solution.py:212
  65.4 3.3 %carry1.1.refs_3_ = f32[32,24,128]{2,1,0:T(8,128)} custom-call(s32[2]{0:T(128)} %pad_add_fusion.refs_0_, f32[64,192]{1,0:T(8,128)} %bitcast.17, f32[2,192,1536]{2,1,0:T(8,128)} %bitcast.13, f32[2,64,1536]{2,1,0:T(8,128)} %bitcast.15), custom_call_target="tpu_custom_call" | custom-call | tf_op jit(solution)/shard_map/carry1/pallas_call | solution.py:85
  68.7 0.0 copy-start.1
  68.7 6.1 %all-to-all-done.4.refs_0_ = f32[8,24,128]{2,1,0:T(8,128)S(1)} async-done(((f32[8,24,128]{2,1,0:T(8,128)}), f32[8,24,128]{2,1,0:T(8,128)S(1)}, u32[]{:S(2)}, u32[]{:S(2)}) %all-to-all-start.4) | async-done | bytes 98336 | tf_op jit(solution)/shard_map/all_to_all | solution.py:212
  74.8 0.7 total.5
  75.4 3.4 %all-to-all-start.5 = ((f32[8,24,128]{2,1,0:T(8,128)}), f32[8,24,128]{2,1,0:T(8,128)S(1)}, u32[]{:S(2)}, u32[]{:S(2)}) async-start(f32[8,24,128]{2,1,0:T(8,128)} %total.5), calls=%async_computation.5 | async-start | bytes 196608 | tf_op jit(solution)/shard_map/all_to_all | solution.py:212
  78.8 0.7 slice_bitcast_fusion.2
  79.5 0.0 copy-start
  79.5 1.7 copy-done
  81.2 0.4 split.4
  81.5 3.0 %all-to-all-done.5.refs_0_ = f32[8,24,128]{2,1,0:T(8,128)S(1)} async-done(((f32[8,24,128]{2,1,0:T(8,128)}), f32[8,24,128]{2,1,0:T(8,128)S(1)}, u32[]{:S(2)}, u32[]{:S(2)}) %all-to-all-start.5) | async-done | bytes 98336 | tf_op jit(solution)/shard_map/all_to_all | solution.py:212
  84.5 0.0 copy-done.1
  84.5 0.8 factor.4
  85.3 13.3 %all_to_all.58.parts_ref = f32[32,24,128]{2,1,0:T(8,128)S(1)} all-to-all(f32[32,24,128]{2,1,0:T(8,128)S(1)} %factor.4), channel_id=1, replica_groups=mesh['z'=8,'y'=4,'x'=4,'c'=2] {'y','x','c'}, dimensions={0} | all-to-all | bytes 786432 | tf_op jit(solution)/shard_map/all_to_all | solution.py:212
  98.7 11.8 %all_to_all.59.refs_0_ = f32[8,24,128]{2,1,0:T(8,128)S(1)} all-to-all(f32[8,24,128]{2,1,0:T(8,128)S(1)} %fold.5), channel_id=1, replica_groups=mesh['z'=8,'y'=4,'x'=4,'c'=2] {'z'}, dimensions={0} | all-to-all | bytes 196608 | tf_op jit(solution)/shard_map/all_to_all | solution.py:212
  110.5 0.7 total.6
  111.2 3.4 %all-to-all-start.8 = ((f32[8,24,128]{2,1,0:T(8,128)}), f32[8,24,128]{2,1,0:T(8,128)S(1)}, u32[]{:S(2)}, u32[]{:S(2)}) async-start(f32[8,24,128]{2,1,0:T(8,128)} %total.6), calls=%async_computation.8 | async-start | bytes 196608 | tf_op jit(solution)/shard_map/all_to_all | solution.py:212
  114.6 1.8 %slice_bitcast_fusion.matrix_ref = f32[1536,384]{1,0:T(8,128)S(1)} fusion(f32[2,1536,384]{2,1,0:T(8,128)} %param.9), kind=kLoop, calls=%fused_computation | loop fusion | bytes 4718592 | tf_op jit(solution)/shard_map/squeeze | solution.py:246
  116.4 0.4 split.5
  116.8 3.5 %all-to-all-done.8.refs_0_ = f32[8,24,128]{2,1,0:T(8,128)S(1)} async-done(((f32[8,24,128]{2,1,0:T(8,128)}), f32[8,24,128]{2,1,0:T(8,128)S(1)}, u32[]{:S(2)}, u32[]{:S(2)}) %all-to-all-start.8) | async-done | bytes 98336 | tf_op jit(solution)/shard_map/all_to_all | solution.py:212
  120.3 1.6 factor.5
  121.9 4.9 %all-to-all-start.9 = ((f32[32,24,128]{2,1,0:T(8,128)}), f32[32,24,128]{2,1,0:T(8,128)S(1)}, u32[]{:S(2)}, u32[]{:S(2)}) async-start(f32[32,24,128]{2,1,0:T(8,128)} %factor.5), calls=%async_computation.9 | async-start | bytes 786432 | tf_op jit(solution)/shard_map/all_to_all | solution.py:212
  126.8 0.7 collective-permute-start
  127.5 0.0 collective-permute-done.refs_1_
  127.5 13.6 %all-to-all-done.9.refs_0_ = f32[32,24,128]{2,1,0:T(8,128)S(1)} async-done(((f32[32,24,128]{2,1,0:T(8,128)}), f32[32,24,128]{2,1,0:T(8,128)S(1)}, u32[]{:S(2)}, u32[]{:S(2)}) %all-to-all-start.9) | async-done | bytes 393248 | tf_op jit(solution)/shard_map/all_to_all | solution.py:212
  141.0 0.1 total.7
  141.1 28.0 %all_to_all.60.gathered_ref = f32[32,48,128]{2,1,0:T(8,128)S(1)} all-to-all(f32[32,48,128]{2,1,0:T(8,128)S(1)} %total.7), channel_id=1, replica_groups=mesh['z'=8,'y'=4,'x'=4,'c'=2] {'z','y'}, dimensions={0} | all-to-all | bytes 1572864 | tf_op jit(solution)/shard_map/all_to_all | solution.py:212
  169.1 0.9 finish.1
  (2 shorter events, 0.0 us)
Async XLA Ops:
  38.1 9.1 %all-to-all-start.2 = ((f32[8,24,128]{2,1,0:T(8,128)}), f32[8,24,128]{2,1,0:T(8,128)S(1)}, u32[]{:S(2)}, u32[]{:S(2)}) async-start(f32[8,24,128]{2,1,0:T(8,128)} %total.4), calls=%async_computation.2 | async-start | bytes 196608 | tf_op jit(solution)/shard_map/all_to_all | solution.py:212
  62.0 12.7 %all-to-all-start.4 = ((f32[8,24,128]{2,1,0:T(8,128)}), f32[8,24,128]{2,1,0:T(8,128)S(1)}, u32[]{:S(2)}, u32[]{:S(2)}) async-start(f32[8,24,128]{2,1,0:T(8,128)} %fold.4), calls=%async_computation.4 | async-start | bytes 196608 | tf_op jit(solution)/shard_map/all_to_all | solution.py:212
  68.7 15.8 %copy-start.1 = (f32[32,24,128]{2,1,0:T(8,128)S(1)}, f32[32,24,128]{2,1,0:T(8,128)}, u32[]{:S(2)}) copy-start(f32[32,24,128]{2,1,0:T(8,128)} %carry1.1.refs_3_) | copy-start | bytes 1179652
  75.4 9.1 %all-to-all-start.5 = ((f32[8,24,128]{2,1,0:T(8,128)}), f32[8,24,128]{2,1,0:T(8,128)S(1)}, u32[]{:S(2)}, u32[]{:S(2)}) async-start(f32[8,24,128]{2,1,0:T(8,128)} %total.5), calls=%async_computation.5 | async-start | bytes 196608 | tf_op jit(solution)/shard_map/all_to_all | solution.py:212
  79.5 1.7 copy-start
  111.2 9.1 %all-to-all-start.8 = ((f32[8,24,128]{2,1,0:T(8,128)}), f32[8,24,128]{2,1,0:T(8,128)S(1)}, u32[]{:S(2)}, u32[]{:S(2)}) async-start(f32[8,24,128]{2,1,0:T(8,128)} %total.6), calls=%async_computation.8 | async-start | bytes 196608 | tf_op jit(solution)/shard_map/all_to_all | solution.py:212
  121.9 19.2 %all-to-all-start.9 = ((f32[32,24,128]{2,1,0:T(8,128)}), f32[32,24,128]{2,1,0:T(8,128)S(1)}, u32[]{:S(2)}, u32[]{:S(2)}) async-start(f32[32,24,128]{2,1,0:T(8,128)} %factor.5), calls=%async_computation.9 | async-start | bytes 786432 | tf_op jit(solution)/shard_map/all_to_all | solution.py:212
  126.8 0.7 collective-permute-start
